TPU v7x, 32 devices: a whole 2x2x4 slice. The times are simulated.
32 devices in a mesh: rep: 4 (over x, core), shard: 8 (over z, y).
Axes of the slice: x: 2, y: 2, z: 4, core: 2. Of those that a mesh axis runs over, the one named last changes fastest.
Arguments:
- tokens: bfloat16 [32, 1024, 768], P(('rep', 'shard')), may hold values from -6 to 6
- cotangent: bfloat16 [32, 1024, 768], P(('rep', 'shard')), may hold values from -6 to 6
- segments: int32 [32, 1024], P(('rep', 'shard')), may hold values from -1 to 7, as said below
- first_pos: int32 [32, 8], P(('rep', 'shard')), may hold values from 0 to 959, as said below
- labels: int32 [32, 8], P(('rep', 'shard')), may hold values from 0 to 2
- query_weight: bfloat16 [768, 768], P('shard'), may hold values from -0.21875 to 0.21875
- key_weight: bfloat16 [768, 768], P('shard'), may hold values from -0.21875 to 0.21875
- value_weight: bfloat16 [768, 768], P('shard'), may hold values from -0.21875 to 0.21875
- out_weight: bfloat16 [768, 768], P('shard'), may hold values from -0.875 to 0.875
- up_weight: bfloat16 [768, 3072], P('shard'), may hold values from -0.21875 to 0.21875
- down_weight: bfloat16 [3072, 768], P('shard'), may hold values from -0.109375 to 0.109375
- pool_weight: bfloat16 [768, 768], P('shard'), may hold values from -0.21875 to 0.21875
- class_weight: bfloat16 [768, 3], P('shard'), may hold values from -0.21875 to 0.21875
- query_bias: bfloat16 [768], P('shard'), may hold values from -3 to 3
- value_bias: bfloat16 [768], P('shard'), may hold values from -3 to 3
- out_bias: bfloat16 [768], P('shard'), may hold values from -3 to 3
- norm1_gain: bfloat16 [768], P('shard'), may hold values from 0.5 to 1.5
- norm1_shift: bfloat16 [768], P('shard'), may hold values from -3 to 3
- up_bias: bfloat16 [3072], P('shard'), may hold values from -3 to 3
- down_bias: bfloat16 [768], P('shard'), may hold values from -3 to 3
- norm2_gain: bfloat16 [768], P('shard'), may hold values from 0.5 to 1.5
- norm2_shift: bfloat16 [768], P('shard'), may hold values from -3 to 3
- pool_bias: bfloat16 [768], P('shard'), may hold values from -3 to 3
- class_bias: bfloat16 [3], replicated, may hold values from -3 to 3
Outputs:
- output: bfloat16 [32, 1024, 768], P(('rep', 'shard'))
- logits: float32 [32, 8, 3], P(('rep', 'shard'))
- input_grad: float32 [32, 1024, 768], P(('rep', 'shard'))
- query_weight_grad: float32 [768, 768], P('shard')
- key_weight_grad: float32 [768, 768], P('shard')
- value_weight_grad: float32 [768, 768], P('shard')
- out_weight_grad: float32 [768, 768], P('shard')
- up_weight_grad: float32 [768, 3072], P('shard')
- down_weight_grad: float32 [3072, 768], P('shard')
- pool_weight_grad: float32 [768, 768], P('shard')
- class_weight_grad: float32 [768, 3], P('shard')
- query_bias_grad: float32 [768], P('shard')
- value_bias_grad: float32 [768], P('shard')
- out_bias_grad: float32 [768], P('shard')
- norm1_gain_grad: float32 [768], P('shard')
- norm1_shift_grad: float32 [768], P('shard')
- up_bias_grad: float32 [3072], P('shard')
- down_bias_grad: float32 [768], P('shard')
- norm2_gain_grad: float32 [768], P('shard')
- norm2_shift_grad: float32 [768], P('shard')
- pool_bias_grad: float32 [768], P('shard')
- class_bias_grad: float32 [3], replicated
- rms: float32 [4], replicated
Inputs may be any that keep to these rules, and one draw needn't show every extreme that they name: `segments`: in each sequence the tokens of documents 0 to 7 come in order, each document one or more tokens, followed by one or more padding tokens numbered -1; document lengths are heavy-tailed. `first_pos`: the first position of each document, consistent with segments, rising within a sequence; the first document starts at 0.
All inputs are finite; a program needn't handle non-finite values.
Results may differ from a plain program's by a relative error of at most 0.017.
Values may be sent and summed in bfloat16 or wider, within the bound.
No kernel may reach another device: no remote copies, remote signals or barrier semaphores. Data moves between devices by JAX's collectives and lax.ppermute only.
A program may use at most 256 MiB of HBM per device.

v0:
```python
from functools import partial
import math

import jax
import jax.numpy as jnp
from jax import lax
from jax.sharding import PartitionSpec as P

epsilon = 1e-12
highest = lax.Precision.HIGHEST


def product(left, right):
    return jnp.dot(left, right, preferred_element_type=jnp.float32)


def product_left(left, right):
    return lax.dot_general(
        left, right, (((0,), (0,)), ((), ())), preferred_element_type=jnp.float32
    )


def product_right(left, right):
    return lax.dot_general(
        left, right, (((1,), (1,)), ((), ())), preferred_element_type=jnp.float32
    )


def norm_forward(value, gain, shift):
    mean_val = jnp.mean(value, axis=-1, keepdims=True)
    centred = value - mean_val
    variance = jnp.mean(centred * centred, axis=-1, keepdims=True)
    inverse = lax.rsqrt(variance + epsilon)
    normal = centred * inverse
    return (normal * gain + shift, normal, inverse)


def norm_backward(grad_out, normal, inverse, gain):
    scaled = grad_out * gain
    grad_in = inverse * (
        scaled
        - jnp.mean(scaled, axis=-1, keepdims=True)
        - normal * jnp.mean(scaled * normal, axis=-1, keepdims=True)
    )
    return (grad_in, jnp.sum(grad_out * normal, axis=0), jnp.sum(grad_out, axis=0))


def block_inputs(
    queries, key_seqs, value_seqs, segments, block_id, block_rows, blocks_per, head_count
):
    seq_count, length, model_width = queries.shape
    head_size = model_width // head_count
    seq_id = block_id // blocks_per
    row_start = block_id % blocks_per * block_rows
    query_block = lax.dynamic_slice(queries, (seq_id, row_start, 0), (1, block_rows, model_width))[
        0
    ]
    key_seq = lax.dynamic_index_in_dim(key_seqs, seq_id, 0, False).reshape(
        length, head_count, head_size
    )
    value_seq = lax.dynamic_index_in_dim(value_seqs, seq_id, 0, False).reshape(
        length, head_count, head_size
    )
    seg_seq = lax.dynamic_index_in_dim(segments, seq_id, 0, False)
    seg_query = lax.dynamic_slice_in_dim(seg_seq, row_start, block_rows)
    scaling = 1.0 / math.sqrt(head_size)
    query_heads = query_block.reshape(block_rows, head_count, head_size)
    scores = (
        jnp.einsum("qhe,khe->hqk", query_heads, key_seq, preferred_element_type=jnp.float32)
        * scaling
    )
    allowed = (seg_query[:, None] == seg_seq[None, :])[None]
    masked = jnp.where(allowed, scores, -1e30)
    return (seq_id, row_start, query_heads, key_seq, value_seq, masked, scaling)


def attention_forward(queries, key_seqs, value_seqs, segments, head_count):
    seq_count, length, model_width = queries.shape
    block_rows = min(512, length)
    blocks_per = length // block_rows

    def one_block(block_id):
        parts_in = block_inputs(
            queries, key_seqs, value_seqs, segments, block_id, block_rows, blocks_per, head_count
        )
        masked = parts_in[5]
        value_seq = parts_in[4]
        row_peak = jnp.max(masked, axis=-1, keepdims=True)
        expo = jnp.exp(masked - row_peak)
        row_total = jnp.sum(expo, axis=-1, keepdims=True)
        weights_low = (expo / row_total).astype(jnp.bfloat16)
        context = jnp.einsum(
            "hqk,khe->qhe", weights_low, value_seq, preferred_element_type=jnp.float32
        )
        return (
            context.reshape(block_rows, model_width).astype(jnp.bfloat16),
            row_peak[..., 0] + jnp.log(row_total[..., 0]),
        )

    block_ids = jnp.arange(seq_count * blocks_per, dtype=jnp.int32)
    context, logsum = lax.map(one_block, block_ids)
    return (context.reshape(seq_count, length, model_width), logsum)


def attention_backward(queries, key_seqs, value_seqs, segments, logsum, grad_context, head_count):
    seq_count, length, model_width = queries.shape
    block_rows = min(512, length)
    blocks_per = length // block_rows
    head_size = model_width // head_count

    def one_block(block_id):
        seq_id, row_start, query_heads, key_seq, value_seq, masked, scaling = block_inputs(
            queries, key_seqs, value_seqs, segments, block_id, block_rows, blocks_per, head_count
        )
        grad_block = lax.dynamic_slice(
            grad_context, (seq_id, row_start, 0), (1, block_rows, model_width)
        )[0]
        grad_heads = grad_block.reshape(block_rows, head_count, head_size)
        logsum_block = lax.dynamic_index_in_dim(logsum, block_id, 0, False)
        probs = jnp.exp(masked - logsum_block[..., None])
        grad_probs = jnp.einsum(
            "qhe,khe->hqk", grad_heads, value_seq, preferred_element_type=jnp.float32
        )
        inner = jnp.sum(grad_probs * probs, axis=-1, keepdims=True)
        grad_scores = (probs * (grad_probs - inner)).astype(jnp.bfloat16)
        grad_query = (
            jnp.einsum("hqk,khe->qhe", grad_scores, key_seq, preferred_element_type=jnp.float32)
            * scaling
        )
        grad_key = (
            jnp.einsum("hqk,qhe->khe", grad_scores, query_heads, preferred_element_type=jnp.float32)
            * scaling
        )
        grad_value = jnp.einsum(
            "hqk,qhe->khe",
            probs.astype(jnp.bfloat16),
            grad_heads,
            preferred_element_type=jnp.float32,
        )
        return (
            grad_query.reshape(block_rows, model_width),
            grad_key.reshape(length, model_width),
            grad_value.reshape(length, model_width),
        )

    block_ids = jnp.arange(seq_count * blocks_per, dtype=jnp.int32)
    grad_query, grad_key, grad_value = lax.map(one_block, block_ids)
    grad_query = grad_query.reshape(seq_count * length, model_width).astype(jnp.bfloat16)
    grad_key = jnp.sum(grad_key.reshape(seq_count, blocks_per, length, model_width), axis=1)
    grad_value = jnp.sum(grad_value.reshape(seq_count, blocks_per, length, model_width), axis=1)
    grad_key = grad_key.reshape(seq_count * length, model_width).astype(jnp.bfloat16)
    grad_value = grad_value.reshape(seq_count * length, model_width).astype(jnp.bfloat16)
    return (grad_query, grad_key, grad_value)


def body(
    tokens,
    cotangent,
    segments,
    first_pos,
    labels,
    query_weight,
    key_weight,
    value_weight,
    out_weight,
    up_weight,
    down_weight,
    pool_weight,
    class_weight,
    query_bias,
    value_bias,
    out_bias,
    norm1_gain,
    norm1_shift,
    up_bias,
    down_bias,
    norm2_gain,
    norm2_shift,
    pool_bias,
    class_bias,
):
    full = (
        lax.all_gather(query_weight, "shard", axis=0, tiled=True),
        lax.all_gather(key_weight, "shard", axis=0, tiled=True),
        lax.all_gather(value_weight, "shard", axis=0, tiled=True),
        lax.all_gather(out_weight, "shard", axis=0, tiled=True),
        lax.all_gather(up_weight, "shard", axis=0, tiled=True),
        lax.all_gather(down_weight, "shard", axis=0, tiled=True),
        lax.all_gather(pool_weight, "shard", axis=0, tiled=True),
        lax.all_gather(class_weight, "shard", axis=0, tiled=True),
        lax.all_gather(query_bias, "shard", axis=0, tiled=True),
        lax.all_gather(value_bias, "shard", axis=0, tiled=True),
        lax.all_gather(out_bias, "shard", axis=0, tiled=True),
        lax.all_gather(norm1_gain, "shard", axis=0, tiled=True),
        lax.all_gather(norm1_shift, "shard", axis=0, tiled=True),
        lax.all_gather(up_bias, "shard", axis=0, tiled=True),
        lax.all_gather(down_bias, "shard", axis=0, tiled=True),
        lax.all_gather(norm2_gain, "shard", axis=0, tiled=True),
        lax.all_gather(norm2_shift, "shard", axis=0, tiled=True),
        lax.all_gather(pool_bias, "shard", axis=0, tiled=True),
    )
    (
        query_full,
        key_full,
        value_full,
        out_full,
        up_full,
        down_full,
        pool_full,
        class_full,
        query_bias_full,
        value_bias_full,
        out_bias_full,
        gain_one_low,
        shift_one_low,
        up_bias_full,
        down_bias_full,
        gain_two_low,
        shift_two_low,
        pool_bias_full,
    ) = full
    gain_one = gain_one_low.astype(jnp.float32)
    gain_two = gain_two_low.astype(jnp.float32)
    seq_count, length, model_width = tokens.shape
    head_count = model_width // 64
    flat_tokens = tokens.reshape(-1, model_width)
    queries = (product(flat_tokens, query_full) + query_bias_full.astype(jnp.float32)).astype(
        jnp.bfloat16
    )
    key_rows = product(flat_tokens, key_full).astype(jnp.bfloat16)
    value_rows = (product(flat_tokens, value_full) + value_bias_full.astype(jnp.float32)).astype(
        jnp.bfloat16
    )
    query_seqs = queries.reshape(seq_count, length, model_width)
    key_seqs = key_rows.reshape(seq_count, length, model_width)
    value_seqs = value_rows.reshape(seq_count, length, model_width)
    context, logsum = attention_forward(query_seqs, key_seqs, value_seqs, segments, head_count)
    context_flat = context.reshape(-1, model_width)
    attended = product(context_flat, out_full) + out_bias_full.astype(jnp.float32)
    first_sum = flat_tokens.astype(jnp.float32) + attended
    normed, normal_one, inverse_one = norm_forward(
        first_sum, gain_one, shift_one_low.astype(jnp.float32)
    )
    normed_low = normed.astype(jnp.bfloat16)
    pre_act = product(normed_low, up_full) + up_bias_full.astype(jnp.float32)
    hidden_low = jax.nn.gelu(pre_act, approximate=False).astype(jnp.bfloat16)
    ffn_out = product(hidden_low, down_full) + down_bias_full.astype(jnp.float32)
    second_sum = normed + ffn_out
    output_f, normal_two, inverse_two = norm_forward(
        second_sum, gain_two, shift_two_low.astype(jnp.float32)
    )
    output_seq = output_f.reshape(seq_count, length, model_width)
    doc_count = first_pos.shape[1]
    picker = (first_pos[:, :, None] == jnp.arange(length, dtype=jnp.int32)[None, None, :]).astype(
        jnp.float32
    )
    picked = jnp.einsum("sjl,slc->sjc", picker, output_seq, precision=highest)
    picked = picked.reshape(-1, model_width).astype(jnp.bfloat16)
    pool_pre = product(picked, pool_full) + pool_bias_full.astype(jnp.float32)
    pool_tanh = jnp.tanh(pool_pre)
    pooled_low = pool_tanh.astype(jnp.bfloat16)
    logits = product(pooled_low, class_full) + class_bias.astype(jnp.float32)
    class_count = class_bias.shape[0]
    class_peak = jnp.max(logits, axis=-1, keepdims=True)
    class_exp = jnp.exp(logits - class_peak)
    class_prob = class_exp / jnp.sum(class_exp, axis=-1, keepdims=True)
    targets = (
        labels.reshape(-1)[:, None] == jnp.arange(class_count, dtype=jnp.int32)[None, :]
    ).astype(jnp.float32)
    grad_logits = class_prob - targets
    grad_class_bias = jnp.sum(grad_logits, axis=0)
    back = (
        lax.all_gather(query_weight, "shard", axis=0, tiled=True),
        lax.all_gather(key_weight, "shard", axis=0, tiled=True),
        lax.all_gather(value_weight, "shard", axis=0, tiled=True),
        lax.all_gather(out_weight, "shard", axis=0, tiled=True),
        lax.all_gather(up_weight, "shard", axis=0, tiled=True),
        lax.all_gather(down_weight, "shard", axis=0, tiled=True),
        lax.all_gather(pool_weight, "shard", axis=0, tiled=True),
        lax.all_gather(class_weight, "shard", axis=0, tiled=True),
        lax.all_gather(norm1_gain, "shard", axis=0, tiled=True),
        lax.all_gather(norm2_gain, "shard", axis=0, tiled=True),
    )
    back_query, back_key, back_value, back_out = (back[0], back[1], back[2], back[3])
    back_up, back_down, back_pool, back_class = (back[4], back[5], back[6], back[7])
    back_gain_one, back_gain_two = (back[8].astype(jnp.float32), back[9].astype(jnp.float32))
    grad_class = jnp.dot(pooled_low.astype(jnp.float32).T, grad_logits, precision=highest)
    grad_pooled = jnp.dot(grad_logits, back_class.astype(jnp.float32).T, precision=highest)
    grad_pool_pre = (grad_pooled * (1.0 - pool_tanh * pool_tanh)).astype(jnp.bfloat16)
    grad_pool_bias = jnp.sum(grad_pool_pre.astype(jnp.float32), axis=0)
    grad_pool = product_left(picked, grad_pool_pre)
    grad_picked = product_right(grad_pool_pre, back_pool).reshape(seq_count, doc_count, model_width)
    grad_output = cotangent.astype(jnp.float32) + jnp.einsum(
        "sjl,sjc->slc", picker, grad_picked, precision=highest
    )
    grad_output = grad_output.reshape(-1, model_width)
    grad_second, grad_gain_two, grad_shift_two = norm_backward(
        grad_output, normal_two, inverse_two, back_gain_two
    )
    grad_ffn = grad_second.astype(jnp.bfloat16)
    grad_down_bias = jnp.sum(grad_ffn.astype(jnp.float32), axis=0)
    grad_down = product_left(hidden_low, grad_ffn)
    grad_hidden = product_right(grad_ffn, back_down)
    unused_value, gelu_back = jax.vjp(partial(jax.nn.gelu, approximate=False), pre_act)
    grad_pre = gelu_back(grad_hidden)[0].astype(jnp.bfloat16)
    grad_up_bias = jnp.sum(grad_pre.astype(jnp.float32), axis=0)
    grad_up = product_left(normed_low, grad_pre)
    grad_normed = grad_second + product_right(grad_pre, back_up)
    grad_first, grad_gain_one, grad_shift_one = norm_backward(
        grad_normed, normal_one, inverse_one, back_gain_one
    )
    grad_attended = grad_first.astype(jnp.bfloat16)
    grad_out_bias = jnp.sum(grad_attended.astype(jnp.float32), axis=0)
    grad_out = product_left(context_flat, grad_attended)
    grad_context = product_right(grad_attended, back_out).astype(jnp.bfloat16)
    grad_queries, grad_keys, grad_values = attention_backward(
        query_seqs,
        key_seqs,
        value_seqs,
        segments,
        logsum,
        grad_context.reshape(seq_count, length, model_width),
        head_count,
    )
    grad_query = product_left(flat_tokens, grad_queries)
    grad_query_bias = jnp.sum(grad_queries.astype(jnp.float32), axis=0)
    grad_key = product_left(flat_tokens, grad_keys)
    grad_value = product_left(flat_tokens, grad_values)
    grad_value_bias = jnp.sum(grad_values.astype(jnp.float32), axis=0)
    input_grad = (
        grad_first
        + product_right(grad_queries, back_query)
        + product_right(grad_keys, back_key)
        + product_right(grad_values, back_value)
    )
    valid = (segments.reshape(-1) >= 0).astype(jnp.float32)
    sums = jnp.stack(
        [
            jnp.sum(valid * jnp.sum(first_sum * first_sum, axis=-1)),
            jnp.sum(valid * jnp.sum(attended * attended, axis=-1)),
            jnp.sum(valid * jnp.sum(second_sum * second_sum, axis=-1)),
            jnp.sum(valid * jnp.sum(ffn_out * ffn_out, axis=-1)),
        ]
    )
    sums_all, valid_all, class_bias_grad = lax.psum(
        (sums, jnp.sum(valid), grad_class_bias), ("rep", "shard")
    )
    rms = jnp.sqrt(sums_all / (valid_all * model_width))
    parts = (
        lax.psum_scatter(grad_query, "shard", scatter_dimension=0, tiled=True),
        lax.psum_scatter(grad_key, "shard", scatter_dimension=0, tiled=True),
        lax.psum_scatter(grad_value, "shard", scatter_dimension=0, tiled=True),
        lax.psum_scatter(grad_out, "shard", scatter_dimension=0, tiled=True),
        lax.psum_scatter(grad_up, "shard", scatter_dimension=0, tiled=True),
        lax.psum_scatter(grad_down, "shard", scatter_dimension=0, tiled=True),
        lax.psum_scatter(grad_pool, "shard", scatter_dimension=0, tiled=True),
        lax.psum_scatter(grad_class, "shard", scatter_dimension=0, tiled=True),
        lax.psum_scatter(grad_query_bias, "shard", scatter_dimension=0, tiled=True),
        lax.psum_scatter(grad_value_bias, "shard", scatter_dimension=0, tiled=True),
        lax.psum_scatter(grad_out_bias, "shard", scatter_dimension=0, tiled=True),
        lax.psum_scatter(grad_gain_one, "shard", scatter_dimension=0, tiled=True),
        lax.psum_scatter(grad_shift_one, "shard", scatter_dimension=0, tiled=True),
        lax.psum_scatter(grad_up_bias, "shard", scatter_dimension=0, tiled=True),
        lax.psum_scatter(grad_down_bias, "shard", scatter_dimension=0, tiled=True),
        lax.psum_scatter(grad_gain_two, "shard", scatter_dimension=0, tiled=True),
        lax.psum_scatter(grad_shift_two, "shard", scatter_dimension=0, tiled=True),
        lax.psum_scatter(grad_pool_bias, "shard", scatter_dimension=0, tiled=True),
    )
    summed = (
        lax.psum(parts[0].astype(jnp.bfloat16), "rep").astype(jnp.float32),
        lax.psum(parts[1].astype(jnp.bfloat16), "rep").astype(jnp.float32),
        lax.psum(parts[2].astype(jnp.bfloat16), "rep").astype(jnp.float32),
        lax.psum(parts[3].astype(jnp.bfloat16), "rep").astype(jnp.float32),
        lax.psum(parts[4].astype(jnp.bfloat16), "rep").astype(jnp.float32),
        lax.psum(parts[5].astype(jnp.bfloat16), "rep").astype(jnp.float32),
        lax.psum(parts[6].astype(jnp.bfloat16), "rep").astype(jnp.float32),
        lax.psum(parts[7].astype(jnp.bfloat16), "rep").astype(jnp.float32),
        lax.psum(parts[8].astype(jnp.bfloat16), "rep").astype(jnp.float32),
        lax.psum(parts[9].astype(jnp.bfloat16), "rep").astype(jnp.float32),
        lax.psum(parts[10].astype(jnp.bfloat16), "rep").astype(jnp.float32),
        lax.psum(parts[11].astype(jnp.bfloat16), "rep").astype(jnp.float32),
        lax.psum(parts[12].astype(jnp.bfloat16), "rep").astype(jnp.float32),
        lax.psum(parts[13].astype(jnp.bfloat16), "rep").astype(jnp.float32),
        lax.psum(parts[14].astype(jnp.bfloat16), "rep").astype(jnp.float32),
        lax.psum(parts[15].astype(jnp.bfloat16), "rep").astype(jnp.float32),
        lax.psum(parts[16].astype(jnp.bfloat16), "rep").astype(jnp.float32),
        lax.psum(parts[17].astype(jnp.bfloat16), "rep").astype(jnp.float32),
    )
    output = output_f.reshape(seq_count, length, model_width).astype(jnp.bfloat16)
    logits_out = logits.reshape(seq_count, doc_count, class_count)
    input_grad = input_grad.reshape(seq_count, length, model_width)
    return (
        output,
        logits_out,
        input_grad,
        summed[0],
        summed[1],
        summed[2],
        summed[3],
        summed[4],
        summed[5],
        summed[6],
        summed[7],
        summed[8],
        summed[9],
        summed[10],
        summed[11],
        summed[12],
        summed[13],
        summed[14],
        summed[15],
        summed[16],
        summed[17],
        class_bias_grad,
        rms,
    )


def solution(mesh):
    return jax.shard_map(
        body,
        mesh=mesh,
        in_specs=(
            P(("rep", "shard"), None, None),
            P(("rep", "shard"), None, None),
            P(("rep", "shard"), None),
            P(("rep", "shard"), None),
            P(("rep", "shard"), None),
            P("shard", None),
            P("shard", None),
            P("shard", None),
            P("shard", None),
            P("shard", None),
            P("shard", None),
            P("shard", None),
            P("shard", None),
            P("shard"),
            P("shard"),
            P("shard"),
            P("shard"),
            P("shard"),
            P("shard"),
            P("shard"),
            P("shard"),
            P("shard"),
            P("shard"),
            P(),
        ),
        out_specs=(
            P(("rep", "shard"), None, None),
            P(("rep", "shard"), None, None),
            P(("rep", "shard"), None, None),
            P("shard", None),
            P("shard", None),
            P("shard", None),
            P("shard", None),
            P("shard", None),
            P("shard", None),
            P("shard", None),
            P("shard", None),
            P("shard"),
            P("shard"),
            P("shard"),
            P("shard"),
            P("shard"),
            P("shard"),
            P("shard"),
            P("shard"),
            P("shard"),
            P("shard"),
            P(),
            P(),
        ),
        check_vma=False,
    )
```

profile of v0, /device:TPU:1, one launch (start us, length us, event | category | flops | bytes accessed | tf_op | source)
XLA Modules:
  0.0 1403.0 jit_solution(1539975271951226048)
XLA Ops:
  23.4 31.4 %all-reduce.21 = (bf16[768]{0:T(1024)(128)(2,1)S(1)}, bf16[768]{0:T(1024)(128)(2,1)S(1)}, bf16[768]{0:T(1024)(128)(2,1)S(1)}, bf16[768]{0:T(1024)(128)(2,1)S(1)}...) all-reduce(bf16[768]{0:T(1024)(128)(2,1)S(1)} %dynamic-update-slice, ...), channel_id=1, replica_groups=mesh['rep'=4,'shard'=8] {'shard'}, use_global_device_ids=true, to_apply=%add | all-reduce | flops 6912 | bytes 27648
  72.7 22.6 %all-gather = bf16[8,1,384]{2,1,0:T(2,128)(2,1)S(1)} all-gather(bf16[1,1,384]{2,1,0:T(2,128)(2,1)S(1)} %reshape.386), channel_id=1, replica_groups=mesh['rep'=4,'shard'=8] {'shard'}, dimensions={0}, use_global_device_ids=true | all-gather | bytes 6912 | tf_op jit(solution)/shard_map/all_gather | solution.py:196
  109.0 27.5 %all-gather.12.cloned.1.call-done = bf16[768,768]{1,0:T(8,128)(2,1)} async-done(((bf16[96,768]{1,0:T(8,128)(2,1)}), bf16[768,768]{1,0:T(8,128)(2,1)}) %all-gather.12.cloned.1.call-update) | async-done | bytes 1179664 | tf_op jit(solution)/shard_map/all_gather | solution.py:184
  143.4 81.9 %while.30 = (s32[]{:T(128)}, bf16[2,512,768]{2,1,0:T(8,128)(2,1)}, f32[2,12,512]{2,1,0:T(8,128)S(1)}, s32[2]{0:T(128)S(1)}, s32[1,1024]{1,0:T(1,128)S(1)}, /*ind...) while((s32[]{:T(128)}, bf16[2,512,768]{2,1,0:T(8,128)(2,1)}, ...), condition=%wide.region_3.4_spmd, body=%wide.region_0.3_spmd.sunk | while | flops 1687021568 | bytes 187926864 | solution.py:101
  232.7 27.0 %all-gather.18.cloned.1.call-done = bf16[768,3072]{1,0:T(8,128)(2,1)} async-done(((bf16[96,3072]{1,0:T(8,128)(2,1)}), bf16[768,3072]{1,0:T(8,128)(2,1)}) %all-gather.18.cloned.1.call-update) | async-done | bytes 4718608 | tf_op jit(solution)/shard_map/all_gather | solution.py:187
  259.8 37.8 %multiply_convert_fusion.1 = (bf16[1024,3072]{1,0:T(8,128)(2,1)}, f32[1024,3072]{1,0:T(8,128)}, f32[1024,3072]{1,0:T(8,128)}) fusion(f32[3072]{0:T(1024)S(1)} %bitcast.232, bf16[768,3072]{1,0:T(8,128)(2,1)} %all-gather.18.cloned.1.call-done, f32[1024,768]{0,1:T(8,128)} %copy-done.3, f32[768]{0:T(1024)S(1)} %copy-done.49, f32[768]{0:T(1024)S(1)} %copy-done.34, ...), kind=kOutput, calls=%fused_computation.36 | convolution fusion | flops 5043388416 | bytes 39348224 | tf_op jit(solution)/shard_map/dot_general | solution.py:14
  297.6 42.0 %all-gather.20.cloned.1.call-done = bf16[3072,768]{1,0:T(8,128)(2,1)} async-done(((bf16[384,768]{1,0:T(8,128)(2,1)}), bf16[3072,768]{1,0:T(8,128)(2,1)}) %all-gather.20.cloned.1.call-update) | async-done | bytes 4718608 | tf_op jit(solution)/shard_map/all_gather | solution.py:188
  352.8 27.9 %all-gather.22.cloned.1.call-done = bf16[768,768]{1,0:T(8,128)(2,1)} async-done(((bf16[96,768]{1,0:T(8,128)(2,1)}), bf16[768,768]{1,0:T(8,128)(2,1)}) %all-gather.22.cloned.1.call-update) | async-done | bytes 1179664 | tf_op jit(solution)/shard_map/all_gather | solution.py:189
  394.8 20.1 %convert_reduce_fusion = (f32[3072]{0:T(1024)}, bf16[1024,3072]{1,0:T(8,128)(2,1)}) fusion(f32[1024,3072]{1,0:T(8,128)} %get-tuple-element.498, bf16[3072,768]{1,0:T(8,128)(2,1)} %all-gather.20.cloned.1.call-done, f32[1024,768]{0,1:T(8,128)} %get-tuple-element.492, f32[1024,3072]{1,0:T(8,128)} %get-tuple-element.512, f32[3072]{0:T(1024)S(1)} %bitcast.233), kind=kOutput, calls=%fused_computation.34 | convolution fusion | flops 4886098944 | bytes 39346176 | tf_op jit(solution)/shard_map/dot_general | solution.py:24
  436.7 202.1 %while.31 = (s32[]{:T(128)}, bf16[2,512,768]{2,1,0:T(8,128)(2,1)}, f32[2,1024,768]{1,2,0:T(8,128)}, f32[2,1024,768]{1,2,0:T(8,128)}, s32[2]{0:T(128)S(1)}, /*ind...) while((s32[]{:T(128)}, bf16[2,512,768]{2,1,0:T(8,128)(2,1)}, ...), condition=%wide.region_16.17_spmd, body=%wide.region_14.16_spmd.sunk | while | flops 4122994688 | bytes 229558672 | solution.py:147
  456.5 13.4 fusion.161
  469.8 20.2 %multiply_reduce_fusion.12 = (f32[12,512]{1,0:T(8,128)S(1)}, f32[12,512,1024]{2,1,0:T(8,128)}) fusion(f32[12,512,1024]{2,1,0:T(8,128)} %fusion.160, f32[12,512]{1,0:T(8,128)S(1)} %dynamic-slice_bitcast_fusion.2, pred[512,1024]{1,0:T(8,128)(4,1)S(1)} %broadcast_compare_fusion.5, bf16[512,12,64]{0,2,1:T(8,128)(2,1)S(1)} %bitcast.222, ...), kind=kOutput, calls=%fused_computation.15.clone.1 | convolution fusion | flops 836757504 | bytes 53264384 | tf_op jit(solution)/shard_map/while/body/eval_jaxpr/qhe,khe->hqk/dot_general | solution.py:121
  490.0 21.5 %multiply_convert_fusion.3 = bf16[12,512,1024]{2,1,0:T(8,128)(2,1)} fusion(f32[12,512,1024]{2,1,0:T(8,128)} %get-tuple-element.647, f32[12,512,1024]{2,1,0:T(8,128)} %fusion.160, f32[12,512]{1,0:T(8,128)S(1)} %get-tuple-element.648, f32[12,512]{1,0:T(8,128)S(1)} %dynamic-slice_bitcast_fusion.2, pred[512,1024]{1,0:T(8,128)(4,1)S(1)} %broadcast_compare_fusion.5), kind=kLoop, calls=%fused_computation.14.clone.1 | loop fusion | flops 37748736 | bytes 63488000 | tf_op jit(solution)/shard_map/while/body/eval_jaxpr/convert_element_type | solution.py:125
  570.4 20.1 %multiply_reduce_fusion.12 = (f32[12,512]{1,0:T(8,128)S(1)}, f32[12,512,1024]{2,1,0:T(8,128)}) fusion(f32[12,512,1024]{2,1,0:T(8,128)} %fusion.160, f32[12,512]{1,0:T(8,128)S(1)} %dynamic-slice_bitcast_fusion.2, pred[512,1024]{1,0:T(8,128)(4,1)S(1)} %broadcast_compare_fusion.5, bf16[512,12,64]{0,2,1:T(8,128)(2,1)S(1)} %bitcast.222, ...), kind=kOutput, calls=%fused_computation.15.clone.1 | convolution fusion | flops 836757504 | bytes 53264384 | tf_op jit(solution)/shard_map/while/body/eval_jaxpr/qhe,khe->hqk/dot_general | solution.py:121
  590.6 21.2 %multiply_convert_fusion.3 = bf16[12,512,1024]{2,1,0:T(8,128)(2,1)} fusion(f32[12,512,1024]{2,1,0:T(8,128)} %get-tuple-element.647, f32[12,512,1024]{2,1,0:T(8,128)} %fusion.160, f32[12,512]{1,0:T(8,128)S(1)} %get-tuple-element.648, f32[12,512]{1,0:T(8,128)S(1)} %dynamic-slice_bitcast_fusion.2, pred[512,1024]{1,0:T(8,128)(4,1)S(1)} %broadcast_compare_fusion.5), kind=kLoop, calls=%fused_computation.14.clone.1 | loop fusion | flops 37748736 | bytes 63488000 | tf_op jit(solution)/shard_map/while/body/eval_jaxpr/convert_element_type | solution.py:125
  703.7 14.1 %reduce-scatter.27.cloned.1.call-done = f32[96,768]{1,0:T(8,128)} async-done(((f32[768,768]{1,0:T(8,128)}), f32[96,768]{1,0:T(8,128)}) %reduce-scatter.27.cloned.1.call-update) | async-done | bytes 294928
  719.6 69.7 %reduce-scatter.29.cloned.1.call-done = f32[96,768]{1,0:T(8,128)} async-done(((f32[768,768]{1,0:T(8,128)}), f32[96,768]{1,0:T(8,128)}) %reduce-scatter.29.cloned.1.call-update) | async-done | bytes 294928
  791.1 69.9 %reduce-scatter.25.cloned.1.call-done = f32[96,768]{1,0:T(8,128)} async-done(((f32[768,768]{1,0:T(8,128)}), f32[96,768]{1,0:T(8,128)}) %reduce-scatter.25.cloned.1.call-update) | async-done | bytes 294928
  862.7 69.6 %reduce-scatter.23.cloned.1.call-done = f32[96,768]{1,0:T(8,128)} async-done(((f32[768,768]{1,0:T(8,128)}), f32[96,768]{1,0:T(8,128)}) %reduce-scatter.23.cloned.1.call-update) | async-done | bytes 294928 | tf_op jit(solution)/shard_map/reduce_scatter | solution.py:356
  934.0 165.6 %reduce-scatter.19.cloned.1.call-done = f32[96,3072]{1,0:T(8,128)} async-done(((f32[768,3072]{1,0:T(8,128)}), f32[96,3072]{1,0:T(8,128)}) %reduce-scatter.19.cloned.1.call-update) | async-done | bytes 1179664 | tf_op jit(solution)/shard_map/reduce_scatter | solution.py:354
  1101.7 163.8 %reduce-scatter.21.cloned.1.call-done = f32[384,768]{1,0:T(8,128)} async-done(((f32[3072,768]{1,0:T(8,128)}), f32[384,768]{1,0:T(8,128)}) %reduce-scatter.21.cloned.1.call-update) | async-done | bytes 1179664 | tf_op jit(solution)/shard_map/reduce_scatter | solution.py:355
  1270.4 39.4 %all-reduce.19 = (f32[3]{0:T(128)}, f32[4]{0:T(128)S(1)}, f32[]{:T(128)}) all-reduce(f32[3]{0:T(128)S(1)} %copy-done.54, f32[4]{0:T(128)S(1)} %pad_maximum_fusion, f32[]{:T(128)} %get-tuple-element.406), channel_id=1, replica_groups=mesh['rep'=4,'shard'=8] {'rep','shard'}, use_global_device_ids=true, to_apply=%region_66.67 | all-reduce | flops 8 | bytes 64 | tf_op jit(solution)/shard_map/psum | solution.py:345
  1312.5 29.3 %all-reduce.20 = (bf16[768]{0:T(1024)(128)(2,1)S(1)}, bf16[768]{0:T(1024)(128)(2,1)S(1)}, bf16[768]{0:T(1024)(128)(2,1)S(1)}, bf16[768]{0:T(1024)(128)(2,1)S(1)}...) all-reduce(f32[768]{0:T(1024)S(1)} %convert_reduce_fusion.4, ...), channel_id=10, replica_groups=mesh['rep'=4,'shard'=8] {'shard'}, use_global_device_ids=true, to_apply=%region_36.37.clone | all-reduce | flops 9984 | bytes 59904
  1357.1 14.5 %all-reduce.22 = (bf16[96,3]{0,1:T(4,128)(2,1)S(1)}, bf16[96]{0:T(256)(128)(2,1)S(1)}, bf16[96]{0:T(256)(128)(2,1)S(1)}, bf16[96]{0:T(256)(128)(2,1)S(1)}, bf16[...) all-reduce(bf16[96,3]{0,1:T(4,128)(2,1)S(1)} %copy.125, ...), channel_id=1, replica_groups=mesh['rep'=4,'shard'=8] {'rep'}, use_global_device_ids=true, to_apply=%region_34.35 | all-reduce | flops 1536 | bytes 6144 | tf_op jit(solution)/shard_map/psum | solution.py:377
  (343 shorter events, 405.5 us)
Async XLA Ops:
  7.2 91.9 %all-gather.14.cloned.1.call-start = ((), (), s32[]{:S(2)}) async-start(), calls=%async_computation.10 | async-start | bytes 1327104 | tf_op jit(solution)/shard_map/all_gather | solution.py:185
  7.9 95.5 %all-gather.10.cloned.1.call-start = ((), (), s32[]{:S(2)}) async-start(), calls=%async_computation.8 | async-start | bytes 1327104 | tf_op jit(solution)/shard_map/all_gather | solution.py:183
  8.7 127.8 %all-gather.12.cloned.1.call-start = ((), (), s32[]{:S(2)}) async-start(), calls=%async_computation.9 | async-start | bytes 1327104 | tf_op jit(solution)/shard_map/all_gather | solution.py:184
  9.4 216.0 %all-gather.16.cloned.1.call-start = ((), (), s32[]{:S(2)}) async-start(), calls=%async_computation.11 | async-start | bytes 1327104 | tf_op jit(solution)/shard_map/all_gather | solution.py:186
  10.0 249.8 %all-gather.18.cloned.1.call-start = ((), (), s32[]{:S(2)}) async-start(), calls=%async_computation.12 | async-start | bytes 5308416 | tf_op jit(solution)/shard_map/all_gather | solution.py:187
  10.6 329.0 %all-gather.20.cloned.1.call-start = ((), (), s32[]{:S(2)}) async-start(), calls=%async_computation.13 | async-start | bytes 5308416 | tf_op jit(solution)/shard_map/all_gather | solution.py:188
  11.2 369.6 %all-gather.22.cloned.1.call-start = ((), (), s32[]{:S(2)}) async-start(), calls=%async_computation.14 | async-start | bytes 1327104 | tf_op jit(solution)/shard_map/all_gather | solution.py:189
  11.9 690.2 %reduce-scatter.17.cloned.1.call-start = ((), (), s32[]{:S(2)}) async-start(), calls=%async_computation.15 | async-start | bytes 2654208 | tf_op jit(solution)/shard_map/reduce_scatter | solution.py:353
  432.1 285.7 %reduce-scatter.27.cloned.1.call-start = ((), (), s32[]{:S(2)}) async-start(), calls=%async_computation.20 | async-start | bytes 2654208
  649.1 140.2 %reduce-scatter.29.cloned.1.call-start = ((), (), s32[]{:S(2)}) async-start(), calls=%async_computation.21 | async-start | bytes 2654208
  659.0 202.0 %reduce-scatter.25.cloned.1.call-start = ((), (), s32[]{:S(2)}) async-start(), calls=%async_computation.19 | async-start | bytes 2654208
  666.5 265.8 %reduce-scatter.23.cloned.1.call-start = ((), (), s32[]{:S(2)}) async-start(), calls=%async_computation.18 | async-start | bytes 2654208 | tf_op jit(solution)/shard_map/reduce_scatter | solution.py:356
  668.6 431.0 %reduce-scatter.19.cloned.1.call-start = ((), (), s32[]{:S(2)}) async-start(), calls=%async_computation.16 | async-start | bytes 10616832 | tf_op jit(solution)/shard_map/reduce_scatter | solution.py:354
  679.4 586.2 %reduce-scatter.21.cloned.1.call-start = ((), (), s32[]{:S(2)}) async-start(), calls=%async_computation.17 | async-start | bytes 10616832 | tf_op jit(solution)/shard_map/reduce_scatter | solution.py:355
  690.2 666.1 %reduce-scatter.31.cloned.1.call-start = ((), (), s32[]{:S(2)}) async-start(), calls=%async_computation.22 | async-start | bytes 442368
  693.4 690.7 %all-reduce.26.cloned.1.call-start = ((), (), s32[]{:S(2)}) async-start(), calls=%async_computation.23 | async-start | bytes 4128768 | tf_op jit(solution)/shard_map/psum | solution.py:370
  862.7 407.7 %copy-start.54 = (f32[3]{0:T(128)S(1)}, f32[3]{0:T(128)}, u32[]{:S(2)}) copy-start(f32[3]{0:T(128)} %get-tuple-element.489) | copy-start | bytes 40
  1101.7 210.8 %copy-start.32 = (f32[768]{0:T(1024)S(1)}, f32[768]{0:T(1024)}, u32[]{:S(2)}) copy-start(f32[768]{0:T(1024)} %get-tuple-element.491) | copy-start | bytes 9220
  1101.7 210.8 %copy-start.33 = (f32[768]{0:T(1024)S(1)}, f32[768]{0:T(1024)}, u32[]{:S(2)}) copy-start(f32[768]{0:T(1024)} %get-tuple-element.493) | copy-start | bytes 9220
  1101.7 210.8 %copy-start.39 = (f32[768]{0:T(1024)S(1)}, f32[768]{0:T(1024)}, u32[]{:S(2)}) copy-start(f32[768]{0:T(1024)} %get-tuple-element.519) | copy-start | bytes 9220
  1101.7 210.8 %copy-start.41 = (f32[3072]{0:T(1024)S(1)}, f32[3072]{0:T(1024)}, u32[]{:S(2)}) copy-start(f32[3072]{0:T(1024)} %get-tuple-element.517) | copy-start | bytes 36868
  1101.7 210.8 %copy-start.42 = (f32[768]{0:T(1024)S(1)}, f32[768]{0:T(1024)}, u32[]{:S(2)}) copy-start(f32[768]{0:T(1024)} %get-tuple-element.397) | copy-start | bytes 9220
  1101.7 210.8 %copy-start.43 = (f32[768]{0:T(1024)S(1)}, f32[768]{0:T(1024)}, u32[]{:S(2)}) copy-start(f32[768]{0:T(1024)} %get-tuple-element.399) | copy-start | bytes 9220
  1101.7 240.8 %copy-start.7 = (bf16[1,1024,768]{1,2,0:T(8,128)(2,1)S(1)}, bf16[1,1024,768]{1,2,0:T(8,128)(2,1)}, u32[]{:S(2)}) copy-start(bf16[1,1024,768]{1,2,0:T(8,128)(2,1)} %get-tuple-element.507) | copy-start | bytes 4718596
  (54 other events, 1550.4 us)
Sparse Core Ops, SparseCore 0:
  10.2 42.1 all-gather.13
  54.6 39.8 all-gather.9
  96.7 39.7 all-gather.11
  138.6 39.8 all-gather.15
  180.5 79.2 all-gather.17
  261.8 77.7 all-gather.19
  341.8 38.9 all-gather.21
  432.2 67.9 reduce-scatter.16
  649.2 68.5 reduce-scatter.26
  721.1 68.1 reduce-scatter.28
  792.8 68.0 reduce-scatter.24
  864.3 67.9 reduce-scatter.22
  935.9 163.5 reduce-scatter.18
  1103.0 162.5 reduce-scatter.20
  1268.7 58.7 reduce-scatter.30
  1331.4 52.6 all-reduce.25
where the time goes:
time: 1410 us; the launch traced here: 1400 us
  waiting for transfers between devices  688 us (49%)
  matrix products  330 us (23%)
  blocking collectives  150 us (11%)
  other arithmetic  117 us (8%)
  local copies, waits for them, and re-layouts  88.1 us (6%)
  between operations  17.8 us (1%)
    reduce_scatter x1, waiting for transfers between devices, body(): lax.psum_scatter(grad_up, 'shard', scatter_dimension=0, tiled=True)  166 us
    reduce_scatter x1, waiting for transfers between devices, body(): lax.psum_scatter(grad_down, 'shard', scatter_dimension=0, tiled=True)  164 us
    unnamed x20, waiting for transfers between devices  158 us
    reduce_scatter x1, waiting for transfers between devices, body(): lax.psum_scatter(grad_pool, 'shard', scatter_dimension=0, tiled=True)  69.6 us
    dot_general x8, matrix products, product(): return jnp.dot(left, right, preferred_element_type=jnp.float32)  65.9 us
    unnamed x2, blocking collectives  60.7 us
    dot_general x7, matrix products, product_right(): lax.dot_general(left, right, (((1,), (1,)), ((), ())), preferred_element_...  52.4 us
    dot_general x4, matrix products, block_inputs(): jnp.einsum('qhe,khe->hqk', query_heads, key_seq, preferred_element_type=j...  47.3 us
  transfers between devices with their start and end apart: 16, of which 11 were waited for; matrix products, arithmetic and copies ran while one was open for 33% of the time, Pallas kernels for 0%

commit v1 on v0

--- a/solution.py
+++ b/solution.py
@@ -153,7 +153,100 @@
     return (grad_query, grad_key, grad_value)
 
 
+def swap(value, axis, size, mask):
+    return lax.ppermute(value, axis, [(i, i ^ mask) for i in range(size)])
+
+
+def swap_both(value, reps, shards, rep_mask, shard_mask):
+    pairs = []
+    for r in range(reps):
+        for s in range(shards):
+            pairs.append((r * shards + s, (r ^ rep_mask) * shards + (s ^ shard_mask)))
+    return lax.ppermute(value, ("rep", "shard"), pairs)
+
+
+def shift(value, shards, steps):
+    return lax.ppermute(value, "shard", [(i, (i + 2 * steps) % shards) for i in range(shards)])
+
+
+def quarter(value, rep_id, reps):
+    rows = value.shape[0] // reps
+    return lax.dynamic_slice_in_dim(value, rep_id * rows, rows, 0)
+
+
+def gather_hops(piece, reps, shards):
+    rep_id = lax.axis_index("rep")
+    shard_id = lax.axis_index("shard")
+    z_id = shard_id // 2
+    column = [piece] + [shift(piece, shards, k) for k in range(1, 4)]
+    column = jnp.stack(column)
+    plane = jnp.stack(
+        [
+            column,
+            swap_both(column, reps, shards, 0, 1),
+            swap_both(column, reps, shards, 2, 0),
+            swap_both(column, reps, shards, 2, 1),
+        ]
+    )
+    other = swap(plane, "rep", reps, 1)
+    every = jnp.stack([plane, other])
+    every = every.reshape((2, 2, 2, 4) + piece.shape)
+    z_order = (z_id - jnp.arange(4)) % 4
+    y_order = (shard_id % 2) ^ jnp.arange(2)
+    x_order = (rep_id // 2) ^ jnp.arange(2)
+    c_order = (rep_id % 2) ^ jnp.arange(2)
+    every = jnp.take(every, z_order, axis=3)
+    every = jnp.take(every, y_order, axis=2)
+    every = jnp.take(every, x_order, axis=1)
+    every = jnp.take(every, c_order, axis=0)
+    every = jnp.transpose(every, (3, 2, 1, 0, 4, 5))
+    return every.reshape((shards, reps) + piece.shape)
+
+
+def reduce_hops(parts, reps, shards):
+    rep_id = lax.axis_index("rep")
+    shard_id = lax.axis_index("shard")
+    z_id, y_id = shard_id // 2, shard_id % 2
+    x_id, c_id = rep_id // 2, rep_id % 2
+    rows, width = parts.shape[2:]
+    f32 = jnp.float32
+    grid = parts.reshape(4, 2, 2, 2, rows, width)
+    theirs = lax.dynamic_index_in_dim(grid, 1 - c_id, 3, False)
+    mine = lax.dynamic_index_in_dim(grid, c_id, 3, False)
+    got = swap(theirs, "rep", reps, 1)
+    total = mine.astype(f32) + got.astype(f32)
+    low = total.astype(jnp.bfloat16)
+
+    def at(value, y, x):
+        value = lax.dynamic_index_in_dim(value, y, 1, False)
+        return lax.dynamic_index_in_dim(value, x, 1, False)
+
+    column = (
+        at(total, y_id, x_id)
+        + swap_both(at(low, 1 - y_id, x_id), reps, shards, 0, 1).astype(f32)
+        + swap_both(at(low, y_id, 1 - x_id), reps, shards, 2, 0).astype(f32)
+        + swap_both(at(low, 1 - y_id, 1 - x_id), reps, shards, 2, 1).astype(f32)
+    )
+    low = column.astype(jnp.bfloat16)
+    result = lax.dynamic_index_in_dim(column, z_id, 0, False)
+    for k in range(1, 4):
+        part = lax.dynamic_index_in_dim(low, (z_id + k) % 4, 0, False)
+        result = result + shift(part, shards, k).astype(f32)
+    return result
+
+
+def gather_reps(piece, reps):
+    rep_id = lax.axis_index("rep")
+    pair = jnp.stack([piece, swap(piece, "rep", reps, 2)])
+    four = jnp.stack([pair, swap(pair, "rep", reps, 1)])
+    four = jnp.take(four, (rep_id % 2) ^ jnp.arange(2), axis=0)
+    four = jnp.take(four, (rep_id // 2) ^ jnp.arange(2), axis=1)
+    return jnp.transpose(four, (1, 0, 2, 3)).reshape((reps,) + piece.shape)
+
+
 def body(
+    reps,
+    shards,
     tokens,
     cotangent,
     segments,
@@ -179,46 +272,56 @@
     pool_bias,
     class_bias,
 ):
-    full = (
-        lax.all_gather(query_weight, "shard", axis=0, tiled=True),
-        lax.all_gather(key_weight, "shard", axis=0, tiled=True),
-        lax.all_gather(value_weight, "shard", axis=0, tiled=True),
-        lax.all_gather(out_weight, "shard", axis=0, tiled=True),
-        lax.all_gather(up_weight, "shard", axis=0, tiled=True),
-        lax.all_gather(down_weight, "shard", axis=0, tiled=True),
-        lax.all_gather(pool_weight, "shard", axis=0, tiled=True),
-        lax.all_gather(class_weight, "shard", axis=0, tiled=True),
-        lax.all_gather(query_bias, "shard", axis=0, tiled=True),
-        lax.all_gather(value_bias, "shard", axis=0, tiled=True),
-        lax.all_gather(out_bias, "shard", axis=0, tiled=True),
-        lax.all_gather(norm1_gain, "shard", axis=0, tiled=True),
-        lax.all_gather(norm1_shift, "shard", axis=0, tiled=True),
-        lax.all_gather(up_bias, "shard", axis=0, tiled=True),
-        lax.all_gather(down_bias, "shard", axis=0, tiled=True),
-        lax.all_gather(norm2_gain, "shard", axis=0, tiled=True),
-        lax.all_gather(norm2_shift, "shard", axis=0, tiled=True),
-        lax.all_gather(pool_bias, "shard", axis=0, tiled=True),
-    )
+    rep_id = lax.axis_index("rep")
+    shard_id = lax.axis_index("shard")
+    model_width = tokens.shape[2]
+    ff_width = up_weight.shape[1]
+    blocks = ff_width // model_width
+    small = (
+        query_bias, value_bias, out_bias, norm1_gain, norm1_shift, up_bias, down_bias,
+        norm2_gain, norm2_shift, pool_bias, class_weight.reshape(-1),
+    )
+    small_sizes = [item.shape[0] for item in small]
+    small_row = jnp.concatenate(small)
+    small_rows = -(-small_row.shape[0] // (8 * model_width)) * 8
+    small_row = jnp.pad(small_row, (0, small_rows * model_width - small_row.shape[0]))
+    small_row = small_row.reshape(small_rows, model_width)
+    rows = query_weight.shape[0] // reps
+    first = jnp.concatenate(
+        [quarter(item, rep_id, reps) for item in (query_weight, key_weight, value_weight)]
+        + [small_row]
+    )
+    fast = shards == 8 and reps == 4
+    if fast:
+        first_all = gather_hops(first, reps, shards)
+    else:
+        first_all = lax.all_gather(first, ("shard", "rep")).reshape((shards, reps) + first.shape)
+    small_all = first_all[:, 0, 3 * rows :].reshape(shards, -1)
+    smalls, start = [], 0
+    for size in small_sizes:
+        smalls.append(small_all[:, start : start + size].reshape(-1))
+        start += size
     (
-        query_full,
-        key_full,
-        value_full,
-        out_full,
-        up_full,
-        down_full,
-        pool_full,
-        class_full,
-        query_bias_full,
-        value_bias_full,
-        out_bias_full,
-        gain_one_low,
-        shift_one_low,
-        up_bias_full,
-        down_bias_full,
-        gain_two_low,
-        shift_two_low,
-        pool_bias_full,
-    ) = full
+        query_bias_full, value_bias_full, out_bias_full, gain_one_low, shift_one_low, up_bias_full,
+        down_bias_full, gain_two_low, shift_two_low, pool_bias_full, class_full,
+    ) = smalls
+    class_full = class_full.reshape(model_width, -1)
+
+    def whole_rows(gathered, begin, count):
+        return gathered[:, :, begin : begin + count].reshape(-1, model_width)
+
+    query_full, key_full, value_full = [whole_rows(first_all, i * rows, rows) for i in range(3)]
+    up_blocks = [up_weight[:, i * model_width : (i + 1) * model_width] for i in range(blocks)]
+    second = jnp.concatenate(
+        [quarter(item, rep_id, reps) for item in [out_weight] + up_blocks + [down_weight, pool_weight]]
+    )
+    second_all = lax.all_gather(second, ("shard", "rep")).reshape((shards, reps) + second.shape)
+    out_full = whole_rows(second_all, 0, rows)
+    up_full = jnp.concatenate(
+        [whole_rows(second_all, (1 + i) * rows, rows) for i in range(blocks)], axis=1
+    )
+    down_full = whole_rows(second_all, (1 + blocks) * rows, blocks * rows)
+    pool_full = whole_rows(second_all, (1 + 2 * blocks) * rows, rows)
     gain_one = gain_one_low.astype(jnp.float32)
     gain_two = gain_two_low.astype(jnp.float32)
     seq_count, length, model_width = tokens.shape
@@ -269,21 +372,9 @@
     ).astype(jnp.float32)
     grad_logits = class_prob - targets
     grad_class_bias = jnp.sum(grad_logits, axis=0)
-    back = (
-        lax.all_gather(query_weight, "shard", axis=0, tiled=True),
-        lax.all_gather(key_weight, "shard", axis=0, tiled=True),
-        lax.all_gather(value_weight, "shard", axis=0, tiled=True),
-        lax.all_gather(out_weight, "shard", axis=0, tiled=True),
-        lax.all_gather(up_weight, "shard", axis=0, tiled=True),
-        lax.all_gather(down_weight, "shard", axis=0, tiled=True),
-        lax.all_gather(pool_weight, "shard", axis=0, tiled=True),
-        lax.all_gather(class_weight, "shard", axis=0, tiled=True),
-        lax.all_gather(norm1_gain, "shard", axis=0, tiled=True),
-        lax.all_gather(norm2_gain, "shard", axis=0, tiled=True),
-    )
-    back_query, back_key, back_value, back_out = (back[0], back[1], back[2], back[3])
-    back_up, back_down, back_pool, back_class = (back[4], back[5], back[6], back[7])
-    back_gain_one, back_gain_two = (back[8].astype(jnp.float32), back[9].astype(jnp.float32))
+    back_query, back_key, back_value, back_out = (query_full, key_full, value_full, out_full)
+    back_up, back_down, back_pool, back_class = (up_full, down_full, pool_full, class_full)
+    back_gain_one, back_gain_two = (gain_one, gain_two)
     grad_class = jnp.dot(pooled_low.astype(jnp.float32).T, grad_logits, precision=highest)
     grad_pooled = jnp.dot(grad_logits, back_class.astype(jnp.float32).T, precision=highest)
     grad_pool_pre = (grad_pooled * (1.0 - pool_tanh * pool_tanh)).astype(jnp.bfloat16)
@@ -346,46 +437,62 @@
         (sums, jnp.sum(valid), grad_class_bias), ("rep", "shard")
     )
     rms = jnp.sqrt(sums_all / (valid_all * model_width))
-    parts = (
-        lax.psum_scatter(grad_query, "shard", scatter_dimension=0, tiled=True),
-        lax.psum_scatter(grad_key, "shard", scatter_dimension=0, tiled=True),
-        lax.psum_scatter(grad_value, "shard", scatter_dimension=0, tiled=True),
-        lax.psum_scatter(grad_out, "shard", scatter_dimension=0, tiled=True),
-        lax.psum_scatter(grad_up, "shard", scatter_dimension=0, tiled=True),
-        lax.psum_scatter(grad_down, "shard", scatter_dimension=0, tiled=True),
-        lax.psum_scatter(grad_pool, "shard", scatter_dimension=0, tiled=True),
-        lax.psum_scatter(grad_class, "shard", scatter_dimension=0, tiled=True),
-        lax.psum_scatter(grad_query_bias, "shard", scatter_dimension=0, tiled=True),
-        lax.psum_scatter(grad_value_bias, "shard", scatter_dimension=0, tiled=True),
-        lax.psum_scatter(grad_out_bias, "shard", scatter_dimension=0, tiled=True),
-        lax.psum_scatter(grad_gain_one, "shard", scatter_dimension=0, tiled=True),
-        lax.psum_scatter(grad_shift_one, "shard", scatter_dimension=0, tiled=True),
-        lax.psum_scatter(grad_up_bias, "shard", scatter_dimension=0, tiled=True),
-        lax.psum_scatter(grad_down_bias, "shard", scatter_dimension=0, tiled=True),
-        lax.psum_scatter(grad_gain_two, "shard", scatter_dimension=0, tiled=True),
-        lax.psum_scatter(grad_shift_two, "shard", scatter_dimension=0, tiled=True),
-        lax.psum_scatter(grad_pool_bias, "shard", scatter_dimension=0, tiled=True),
-    )
-    summed = (
-        lax.psum(parts[0].astype(jnp.bfloat16), "rep").astype(jnp.float32),
-        lax.psum(parts[1].astype(jnp.bfloat16), "rep").astype(jnp.float32),
-        lax.psum(parts[2].astype(jnp.bfloat16), "rep").astype(jnp.float32),
-        lax.psum(parts[3].astype(jnp.bfloat16), "rep").astype(jnp.float32),
-        lax.psum(parts[4].astype(jnp.bfloat16), "rep").astype(jnp.float32),
-        lax.psum(parts[5].astype(jnp.bfloat16), "rep").astype(jnp.float32),
-        lax.psum(parts[6].astype(jnp.bfloat16), "rep").astype(jnp.float32),
-        lax.psum(parts[7].astype(jnp.bfloat16), "rep").astype(jnp.float32),
-        lax.psum(parts[8].astype(jnp.bfloat16), "rep").astype(jnp.float32),
-        lax.psum(parts[9].astype(jnp.bfloat16), "rep").astype(jnp.float32),
-        lax.psum(parts[10].astype(jnp.bfloat16), "rep").astype(jnp.float32),
-        lax.psum(parts[11].astype(jnp.bfloat16), "rep").astype(jnp.float32),
-        lax.psum(parts[12].astype(jnp.bfloat16), "rep").astype(jnp.float32),
-        lax.psum(parts[13].astype(jnp.bfloat16), "rep").astype(jnp.float32),
-        lax.psum(parts[14].astype(jnp.bfloat16), "rep").astype(jnp.float32),
-        lax.psum(parts[15].astype(jnp.bfloat16), "rep").astype(jnp.float32),
-        lax.psum(parts[16].astype(jnp.bfloat16), "rep").astype(jnp.float32),
-        lax.psum(parts[17].astype(jnp.bfloat16), "rep").astype(jnp.float32),
-    )
+    low = jnp.bfloat16
+
+    def by_piece(grad):
+        return grad.astype(low).reshape(shards, reps, -1, model_width)
+
+    def scatter(parts_in):
+        rows_in = parts_in.shape[2]
+        flat = parts_in.reshape(-1, model_width)
+        return lax.psum_scatter(flat, ("shard", "rep"), scatter_dimension=0, tiled=True)
+
+    down_part = scatter(jnp.concatenate([by_piece(grad_down), by_piece(grad_pool)], axis=2))
+    up_grads = [by_piece(grad_up[:, i * model_width : (i + 1) * model_width]) for i in range(blocks)]
+    up_part = scatter(jnp.concatenate(up_grads + [by_piece(grad_out)], axis=2))
+    small_grads = (
+        grad_query_bias, grad_value_bias, grad_out_bias, grad_gain_one, grad_shift_one,
+        grad_up_bias, grad_down_bias, grad_gain_two, grad_shift_two, grad_pool_bias,
+        grad_class.reshape(-1),
+    )
+    small_grad = jnp.concatenate([item.reshape(shards, -1) for item in small_grads], axis=1)
+    small_grad = jnp.pad(
+        small_grad, ((0, 0), (0, small_rows * model_width - small_grad.shape[1]))
+    ).astype(low).reshape(shards, 1, small_rows, model_width)
+    small_grad = jnp.broadcast_to(small_grad, (shards, reps, small_rows, model_width))
+    last = jnp.concatenate(
+        [by_piece(grad_query), by_piece(grad_key), by_piece(grad_value), small_grad], axis=2
+    )
+    if fast:
+        last_part = reduce_hops(last, reps, shards)
+    else:
+        last_part = scatter(last).astype(jnp.float32)
+    small_out = last_part[3 * rows :].reshape(-1)
+    final = jnp.concatenate([last_part[: 3 * rows].astype(low), down_part, up_part])
+    if fast:
+        final_all = gather_reps(final, reps)
+    else:
+        final_all = lax.all_gather(final, "rep")
+    final_all = final_all.astype(jnp.float32)
+
+    def own_rows(begin, count):
+        return final_all[:, begin : begin + count].reshape(-1, model_width)
+
+    down_at = 3 * rows
+    up_at = down_at + (blocks + 1) * rows
+    summed = [own_rows(i * rows, rows) for i in range(3)]
+    summed.append(own_rows(up_at + blocks * rows, rows))
+    summed.append(
+        jnp.concatenate([own_rows(up_at + i * rows, rows) for i in range(blocks)], axis=1)
+    )
+    summed.append(own_rows(down_at, blocks * rows))
+    summed.append(own_rows(down_at + blocks * rows, rows))
+    small_parts, start = [], 0
+    for size in small_sizes:
+        small_parts.append(small_out[start : start + size])
+        start += size
+    summed.append(small_parts[-1].reshape(class_weight.shape))
+    summed.extend(small_parts[:-1])
     output = output_f.reshape(seq_count, length, model_width).astype(jnp.bfloat16)
     logits_out = logits.reshape(seq_count, doc_count, class_count)
     input_grad = input_grad.reshape(seq_count, length, model_width)
@@ -418,7 +525,7 @@
 
 def solution(mesh):
     return jax.shard_map(
-        body,
+        partial(body, mesh.shape["rep"], mesh.shape["shard"]),
         mesh=mesh,
         in_specs=(
             P(("rep", "shard"), None, None),

time: 1410 us -> 738 us (0.52)
  waiting for transfers between devices: 688 us -> 59 us
  blocking collectives: 150 us -> 43.6 us
  local copies, waits for them, and re-layouts: 88.1 us -> 130 us
  starting transfers between devices: 0.64 us -> 37.2 us
  matrix products: 330 us -> 306 us
    reduce_scatter x4 -> x2, waiting for transfers between devices: 399 us -> 0.04 us  [scatter(): lax.psum_scatter(flat, ('shard', 'rep'), scatter_dimension=0, tiled=True)]
    unnamed x20 -> x3, waiting for transfers between devices: 158 us -> 0.05 us
    all_gather x7 -> x1, waiting for transfers between devices: 125 us -> 0.01 us  [body(): lax.all_gather(second, ('shard', 'rep'))]
    unnamed x2 -> x0, blocking collectives: 60.7 us -> none
    ppermute x0 -> x16, waiting for transfers between devices: none -> 58.9 us  [the longest x6 42.6 us: swap_both(): return lax.ppermute(value, ('rep', 'shard'), pairs)]
    ppermute x0 -> x16, starting transfers between devices: none -> 37.1 us  [the longest x6 16.5 us: shift(): lax.ppermute(value, 'shard', [(i, (i + 2 * steps) % shards) for i in rang...]
    all_gather x2 -> x0, blocking collectives: 35.7 us -> none  [the longest x1 22.6 us: body(): lax.all_gather(up_bias, 'shard', axis=0, tiled=True)]
    gather x0 -> x6, local copies, waits for them, and re-layouts: none -> 24.1 us  [the longest x1 5.52 us: gather_hops(): every = jnp.take(every, z_order, axis=3)]
  transfers between devices with their start and end apart: 16 -> 19, of which waited for: 11 -> 9; matrix products, arithmetic and copies ran while one was open for 33% -> 59% of each run, Pallas kernels for 0% -> 0%
where the time goes in v1:
time: 738 us; the launch traced here: 733 us
  matrix products  306 us (41%)
  local copies, waits for them, and re-layouts  130 us (18%)
  other arithmetic  130 us (18%)
  waiting for transfers between devices  59 us (8%)
  blocking collectives  43.6 us (6%)
  starting transfers between devices  37.2 us (5%)
  between operations  15.7 us (2%)
  loops' own time  11.5 us (2%)
    dot_general x8, matrix products, product(): return jnp.dot(left, right, preferred_element_type=jnp.float32)  69.2 us
    dot_general x4, matrix products, block_inputs(): jnp.einsum('qhe,khe->hqk', query_heads, key_seq, preferred_element_type=j...  47.4 us
    convert_element_type x2, other arithmetic, one_block(): grad_scores = (probs * (grad_probs - inner)).astype(jnp.bfloat16)  43.7 us
    psum x1, blocking collectives, body(): lax.psum((sums, jnp.sum(valid), grad_class_bias), ('rep', 'shard'))  43.6 us
    ppermute x6, waiting for transfers between devices, swap_both(): return lax.ppermute(value, ('rep', 'shard'), pairs)  42.6 us
    dot_general x7, matrix products, product_right(): lax.dot_general(left, right, (((1,), (1,)), ((), ())), preferred_element_...  41.9 us
    dot_general x2, matrix products, one_block(): jnp.einsum('qhe,khe->hqk', grad_heads, value_seq, preferred_element_type=...  41.1 us
    dot_general x2, matrix products, one_block(): jnp.einsum('hqk,qhe->khe', probs.astype(jnp.bfloat16), grad_heads, prefer...  27.5 us
  transfers between devices with their start and end apart: 19, of which 9 were waited for; matrix products, arithmetic and copies ran while one was open for 59% of the time, Pallas kernels for 0%

profile of v1, /device:TPU:1, one launch (start us, length us, event | category | flops | bytes accessed | tf_op | source)
XLA Modules:
  0.0 733.0 jit_solution(350187922407670964)
XLA Ops:
  45.4 13.8 %collective-permute-done.5 = bf16[4,80,768]{2,1,0:T(8,128)(2,1)S(1)} collective-permute-done((bf16[4,80,768]{2,1,0:T(8,128)(2,1)S(1)}, bf16[4,80,768]{2,1,0:T(8,128)(2,1)S(1)}, u32[]{:S(2)}, u32[]{:S(2)}) %collective-permute-start.5) | collective-permute-done | bytes 491552 | tf_op jit(solution)/shard_map/ppermute | solution.py:165
  59.5 12.4 %collective-permute-start.6 = (bf16[4,4,80,768]{3,2,1,0:T(8,128)(2,1)S(1)}, bf16[4,4,80,768]{3,2,1,0:T(8,128)(2,1)}, u32[]{:S(2)}, u32[]{:S(2)}) collective-permute-start(bf16[4,4,80,768]{3,2,1,0:T(8,128)(2,1)S(1)} %pad_maximum_fusion.4), channel_id=1, source_target_pairs={{0,8},{8,0},{16,24},{24,16},{1,9},{9,1},{17,25},{25,17},{2,10},{10... | collective-permute-start | bytes 5898248 | tf_op jit(solution)/shard_map/ppermute | solution.py:157
  136.8 81.7 %while.30 = (s32[]{:T(128)}, bf16[2,512,768]{2,1,0:T(8,128)(2,1)}, f32[2,12,512]{2,1,0:T(8,128)S(1)}, s32[2]{0:T(128)S(1)}, s32[1,1024]{1,0:T(1,128)S(1)}, /*ind...) while((s32[]{:T(128)}, bf16[2,512,768]{2,1,0:T(8,128)(2,1)}, ...), condition=%wide.region_3.4_spmd, body=%wide.region_0.3_spmd.sunk | while | flops 1687021568 | bytes 187926864 | solution.py:101
  140.1 12.1 %fusion.179 = (f32[12,512]{1,0:T(8,128)S(1)}, f32[12,512,1024]{2,1,0:T(8,128)}) fusion(pred[512,1024]{1,0:T(8,128)(4,1)S(1)} %broadcast_compare_fusion.4, bf16[512,12,64]{0,2,1:T(8,128)(2,1)S(1)} %bitcast.328, bf16[1024,12,64]{0,2,1:T(8,128)(2,1)} %bitcast.303), kind=kOutput, calls=%fused_computation.9.clone.1 | convolution fusion | flops 824174592 | bytes 28073984 | tf_op jit(solution)/shard_map/while/body/eval_jaxpr/qhe,khe->hqk/dot_general | solution.py:69
  152.2 12.3 %fusion.180 = f32[12,512]{1,0:T(8,128)S(1)} fusion(f32[12,512,1024]{2,1,0:T(8,128)} %get-tuple-element.706, f32[12,512]{1,0:T(8,128)S(1)} %get-tuple-element.707, pred[512,1024]{1,0:T(8,128)(4,1)S(1)} %broadcast_compare_fusion.4), kind=kLoop, calls=%fused_computation.10.clone.1 | loop fusion | flops 25159680 | bytes 25739264 | tf_op jit(solution)/shard_map/while/body/eval_jaxpr/reduce_sum | solution.py:90
  167.5 9.0 %fusion.181 = bf16[12,512,64]{1,2,0:T(8,128)(2,1)S(1)} fusion(bf16[1024,12,64]{0,2,1:T(8,128)(2,1)} %bitcast.298, f32[12,512,1024]{2,1,0:T(8,128)S(1)} %copy-done.2, f32[12,512]{1,0:T(8,128)S(1)} %fusion.180, f32[12,512]{1,0:T(8,128)S(1)} %get-tuple-element.707, pred[512,1024]{1,0:T(8,128)(4,1)S(1)} %broadcast_compare_fusion.4), kind=kOutput, calls=%fused_computation.12.clone.1 | convolution fusion | flops 837156864 | bytes 28098560 | tf_op jit(solution)/shard_map/while/body/eval_jaxpr/hqk,khe->qhe/dot_general | solution.py:92
  180.8 12.1 %fusion.179 = (f32[12,512]{1,0:T(8,128)S(1)}, f32[12,512,1024]{2,1,0:T(8,128)}) fusion(pred[512,1024]{1,0:T(8,128)(4,1)S(1)} %broadcast_compare_fusion.4, bf16[512,12,64]{0,2,1:T(8,128)(2,1)S(1)} %bitcast.328, bf16[1024,12,64]{0,2,1:T(8,128)(2,1)} %bitcast.303), kind=kOutput, calls=%fused_computation.9.clone.1 | convolution fusion | flops 824174592 | bytes 28073984 | tf_op jit(solution)/shard_map/while/body/eval_jaxpr/qhe,khe->hqk/dot_general | solution.py:69
  192.9 12.3 %fusion.180 = f32[12,512]{1,0:T(8,128)S(1)} fusion(f32[12,512,1024]{2,1,0:T(8,128)} %get-tuple-element.706, f32[12,512]{1,0:T(8,128)S(1)} %get-tuple-element.707, pred[512,1024]{1,0:T(8,128)(4,1)S(1)} %broadcast_compare_fusion.4), kind=kLoop, calls=%fused_computation.10.clone.1 | loop fusion | flops 25159680 | bytes 25739264 | tf_op jit(solution)/shard_map/while/body/eval_jaxpr/reduce_sum | solution.py:90
  232.3 51.1 %multiply_convert_fusion.1 = (bf16[1024,3072]{1,0:T(8,128)(2,1)}, f32[1024,3072]{1,0:T(8,128)}, f32[1024,3072]{1,0:T(8,128)}) fusion(f32[3072]{0:T(1024)S(1)} %copy-done.55, bf16[768,768]{1,0:T(8,128)(2,1)S(1)} %bitcast.357, bf16[768,768]{1,0:T(8,128)(2,1)S(1)} %bitcast.359, bf16[768,768]{1,0:T(8,128)(2,1)S(1)} %bitcast.361, ...), kind=kOutput, calls=%fused_computation.41 | convolution fusion | flops 5062262784 | bytes 39348224 | tf_op jit(solution)/shard_map/dot_general | solution.py:14
  314.0 19.4 %fusion.106 = (bf16[3072]{0:T(1024)(128)(2,1)}, bf16[1024,3072]{1,0:T(8,128)(2,1)}) fusion(f32[1024,3072]{1,0:T(8,128)} %get-tuple-element.509, bf16[3072,768]{1,0:T(8,128)(2,1)} %bitcast.349, f32[1024,768]{0,1:T(8,128)} %copy-done.15, f32[1024,3072]{1,0:T(8,128)} %get-tuple-element.579, f32[3072]{0:T(1024)S(1)} %copy-done.55), kind=kOutput, calls=%fused_computation.262 | convolution fusion | flops 4882953216 | bytes 39340032 | tf_op jit(solution)/shard_map/dot_general | solution.py:24
  346.0 9.7 %multiply_reduce_fusion.5 = (bf16[768]{0:T(1024)(128)(2,1)}, f32[1024]{0:T(1024)S(1)}, f32[1024]{0:T(1024)S(1)}, f32[1024]{0:T(1024)}, bf16[768]{0:T(1024)(128)(2,1)}, /*index=5*/f32[1024,768]{0,1:T(8,128)S(1)}) fusion(f32[1024,768]{0,1:T(8,128)S(1)} %get-tuple-element.511, f32[1024]{0:T(1024)S(1)} %add_rsqrt_fusion.1, ...), kind=kOutput, calls=%fused_computation.74 | convolution fusion | flops 4860144640 | bytes 20473856 | tf_op jit(solution)/shard_map/dot_general | solution.py:24
  363.6 206.3 %while.31 = (s32[]{:T(128)}, bf16[2,512,768]{2,1,0:T(8,128)(2,1)}, f32[2,1024,768]{1,2,0:T(8,128)}, f32[2,1024,768]{1,2,0:T(8,128)}, s32[2]{0:T(128)S(1)}, /*ind...) while((s32[]{:T(128)}, bf16[2,512,768]{2,1,0:T(8,128)(2,1)}, ...), condition=%wide.region_16.17_spmd, body=%wide.region_14.16_spmd.sunk | while | flops 4122994688 | bytes 229558672 | solution.py:147
  372.1 11.6 %fusion.192 = f32[12,512,1024]{2,1,0:T(8,128)} fusion(bf16[512,12,64]{0,2,1:T(8,128)(2,1)S(1)} %bitcast.326, bf16[1024,12,64]{0,2,1:T(8,128)(2,1)} %bitcast.317), kind=kOutput, calls=%fused_computation.265.clone.1 | convolution fusion | flops 805306368 | bytes 27525120 | tf_op jit(solution)/shard_map/while/body/eval_jaxpr/qhe,khe->hqk/dot_general | solution.py:69
  383.7 13.6 %fusion.193 = f32[12,64,1024]{2,1,0:T(8,128)} fusion(bf16[512,12,64]{0,2,1:T(8,128)(2,1)S(1)} %bitcast.330, f32[12,512,1024]{2,1,0:T(8,128)} %fusion.192, f32[12,512]{1,0:T(8,128)S(1)} %dynamic-slice_bitcast_fusion.9, pred[512,1024]{1,0:T(8,128)(4,1)S(1)} %broadcast_compare_fusion.5), kind=kOutput, calls=%fused_computation.24.clone.1 | convolution fusion | flops 830472192 | bytes 29646848 | tf_op jit(solution)/shard_map/while/body/eval_jaxpr/hqk,qhe->khe/dot_general | solution.py:134
  397.3 20.6 %multiply_reduce_fusion.12 = (f32[12,512]{1,0:T(8,128)S(1)}, f32[12,512,1024]{2,1,0:T(8,128)}) fusion(f32[12,512,1024]{2,1,0:T(8,128)} %fusion.192, f32[12,512]{1,0:T(8,128)S(1)} %dynamic-slice_bitcast_fusion.9, pred[512,1024]{1,0:T(8,128)(4,1)S(1)} %broadcast_compare_fusion.5, bf16[512,12,64]{0,2,1:T(8,128)(2,1)S(1)} %bitcast.331, ...), kind=kOutput, calls=%fused_computation.21.clone.1 | convolution fusion | flops 836757504 | bytes 53264384 | tf_op jit(solution)/shard_map/while/body/eval_jaxpr/qhe,khe->hqk/dot_general | solution.py:121
  417.9 21.6 %multiply_convert_fusion.3 = bf16[12,512,1024]{2,1,0:T(8,128)(2,1)} fusion(f32[12,512,1024]{2,1,0:T(8,128)} %get-tuple-element.719, f32[12,512,1024]{2,1,0:T(8,128)} %fusion.192, f32[12,512]{1,0:T(8,128)S(1)} %get-tuple-element.720, f32[12,512]{1,0:T(8,128)S(1)} %dynamic-slice_bitcast_fusion.9, pred[512,1024]{1,0:T(8,128)(4,1)S(1)} %broadcast_compare_fusion.5), kind=kLoop, calls=%fused_computation.20.clone.1 | loop fusion | flops 37748736 | bytes 63488000 | tf_op jit(solution)/shard_map/while/body/eval_jaxpr/convert_element_type | solution.py:125
  439.4 9.9 %convolution_multiply_fusion.5 = bf16[12,512,64]{1,2,0:T(8,128)(2,1)} fusion(bf16[12,512,1024]{2,1,0:T(8,128)(2,1)} %multiply_convert_fusion.3, bf16[1024,12,64]{0,2,1:T(8,128)(2,1)} %bitcast.317), kind=kOutput, calls=%fused_computation.27.clone.1 | convolution fusion | flops 806092800 | bytes 14942208 | tf_op jit(solution)/shard_map/while/body/eval_jaxpr/hqk,khe->qhe/dot_general | solution.py:127
  474.7 11.6 %fusion.192 = f32[12,512,1024]{2,1,0:T(8,128)} fusion(bf16[512,12,64]{0,2,1:T(8,128)(2,1)S(1)} %bitcast.326, bf16[1024,12,64]{0,2,1:T(8,128)(2,1)} %bitcast.317), kind=kOutput, calls=%fused_computation.265.clone.1 | convolution fusion | flops 805306368 | bytes 27525120 | tf_op jit(solution)/shard_map/while/body/eval_jaxpr/qhe,khe->hqk/dot_general | solution.py:69
  486.4 14.0 %fusion.193 = f32[12,64,1024]{2,1,0:T(8,128)} fusion(bf16[512,12,64]{0,2,1:T(8,128)(2,1)S(1)} %bitcast.330, f32[12,512,1024]{2,1,0:T(8,128)} %fusion.192, f32[12,512]{1,0:T(8,128)S(1)} %dynamic-slice_bitcast_fusion.9, pred[512,1024]{1,0:T(8,128)(4,1)S(1)} %broadcast_compare_fusion.5), kind=kOutput, calls=%fused_computation.24.clone.1 | convolution fusion | flops 830472192 | bytes 29646848 | tf_op jit(solution)/shard_map/while/body/eval_jaxpr/hqk,qhe->khe/dot_general | solution.py:134
  500.3 20.5 %multiply_reduce_fusion.12 = (f32[12,512]{1,0:T(8,128)S(1)}, f32[12,512,1024]{2,1,0:T(8,128)}) fusion(f32[12,512,1024]{2,1,0:T(8,128)} %fusion.192, f32[12,512]{1,0:T(8,128)S(1)} %dynamic-slice_bitcast_fusion.9, pred[512,1024]{1,0:T(8,128)(4,1)S(1)} %broadcast_compare_fusion.5, bf16[512,12,64]{0,2,1:T(8,128)(2,1)S(1)} %bitcast.331, ...), kind=kOutput, calls=%fused_computation.21.clone.1 | convolution fusion | flops 836757504 | bytes 53264384 | tf_op jit(solution)/shard_map/while/body/eval_jaxpr/qhe,khe->hqk/dot_general | solution.py:121
  520.8 22.2 %multiply_convert_fusion.3 = bf16[12,512,1024]{2,1,0:T(8,128)(2,1)} fusion(f32[12,512,1024]{2,1,0:T(8,128)} %get-tuple-element.719, f32[12,512,1024]{2,1,0:T(8,128)} %fusion.192, f32[12,512]{1,0:T(8,128)S(1)} %get-tuple-element.720, f32[12,512]{1,0:T(8,128)S(1)} %dynamic-slice_bitcast_fusion.9, pred[512,1024]{1,0:T(8,128)(4,1)S(1)} %broadcast_compare_fusion.5), kind=kLoop, calls=%fused_computation.20.clone.1 | loop fusion | flops 37748736 | bytes 63488000 | tf_op jit(solution)/shard_map/while/body/eval_jaxpr/convert_element_type | solution.py:125
  542.9 9.9 %convolution_multiply_fusion.5 = bf16[12,512,64]{1,2,0:T(8,128)(2,1)} fusion(bf16[12,512,1024]{2,1,0:T(8,128)(2,1)} %multiply_convert_fusion.3, bf16[1024,12,64]{0,2,1:T(8,128)(2,1)} %bitcast.317), kind=kOutput, calls=%fused_computation.27.clone.1 | convolution fusion | flops 806092800 | bytes 14942208 | tf_op jit(solution)/shard_map/while/body/eval_jaxpr/hqk,khe->qhe/dot_general | solution.py:127
  603.2 20.9 %collective-permute-done.8 = bf16[4,80,768]{2,1,0:T(8,128)(2,1)} collective-permute-done((bf16[4,80,768]{2,1,0:T(8,128)(2,1)}, bf16[4,80,768]{2,1,0:T(8,128)(2,1)}, u32[]{:S(2)}, u32[]{:S(2)}) %collective-permute-start.8) | collective-permute-done | bytes 491552 | tf_op jit(solution)/shard_map/ppermute | solution.py:165
  649.4 43.6 %all-reduce.2 = (f32[3]{0:T(128)}, f32[4]{0:T(128)S(1)}, f32[]{:T(128)}) all-reduce(f32[3]{0:T(128)S(1)} %copy-done.78, f32[4]{0:T(128)S(1)} %pad_maximum_fusion.13, f32[]{:T(128)} %get-tuple-element.450), channel_id=1, replica_groups=mesh['rep'=4,'shard'=8] {'rep','shard'}, use_global_device_ids=true, to_apply=%region_32.33 | all-reduce | flops 8 | bytes 64 | tf_op jit(solution)/shard_map/psum | solution.py:436
  (417 shorter events, 321.8 us)
Async XLA Ops:
  7.2 211.3 %all-gather.3.cloned.1.call-start = ((), (), s32[]{:S(2)}) async-start(), calls=%async_computation.4 | async-start | bytes 12165120 | tf_op jit(solution)/shard_map/all_gather | solution.py:318
  11.8 632.7 %reduce-scatter.3.cloned.1.call-start = ((), (), s32[]{:S(2)}) async-start(), calls=%async_computation.2 | async-start | bytes 6082560 | tf_op jit(solution)/shard_map/reduce_scatter | solution.py:448
  20.5 12.6 %collective-permute-start.1 = (bf16[80,768]{1,0:T(8,128)(2,1)S(1)}, bf16[80,768]{1,0:T(8,128)(2,1)S(1)}, u32[]{:S(2)}, u32[]{:S(2)}) collective-permute-start(bf16[80,768]{1,0:T(8,128)(2,1)S(1)} %get-tuple-element.560), channel_id=1, source_target_pairs={{0,4},{1,5},{2,6},{3,7},{4,0},{5,1},{6,2},{7,3},{8,12},{9,13},{10,... | collective-permute-start | bytes 368648 | tf_op jit(solution)/shard_map/ppermute | solution.py:169
  23.7 9.4 %collective-permute-start = (bf16[80,768]{1,0:T(8,128)(2,1)S(1)}, bf16[80,768]{1,0:T(8,128)(2,1)S(1)}, u32[]{:S(2)}, u32[]{:S(2)}) collective-permute-start(bf16[80,768]{1,0:T(8,128)(2,1)S(1)} %get-tuple-element.560), channel_id=1, source_target_pairs={{0,2},{1,3},{2,4},{3,5},{4,6},{5,7},{6,0},{7,1},{8,10},{9,11},{10,... | collective-permute-start | bytes 368648 | tf_op jit(solution)/shard_map/ppermute | solution.py:169
  25.0 10.3 %collective-permute-start.2 = (bf16[80,768]{1,0:T(8,128)(2,1)S(1)}, bf16[80,768]{1,0:T(8,128)(2,1)S(1)}, u32[]{:S(2)}, u32[]{:S(2)}) collective-permute-start(bf16[80,768]{1,0:T(8,128)(2,1)S(1)} %get-tuple-element.560), channel_id=1, source_target_pairs={{0,6},{1,7},{2,0},{3,1},{4,2},{5,3},{6,4},{7,5},{8,14},{9,15},{10,... | collective-permute-start | bytes 368648 | tf_op jit(solution)/shard_map/ppermute | solution.py:169
  35.4 8.7 %collective-permute-start.4 = (bf16[4,80,768]{2,1,0:T(8,128)(2,1)S(1)}, bf16[4,80,768]{2,1,0:T(8,128)(2,1)S(1)}, u32[]{:S(2)}, u32[]{:S(2)}) collective-permute-start(bf16[4,80,768]{2,1,0:T(8,128)(2,1)S(1)} %get-tuple-element.556), channel_id=1, source_target_pairs={{0,16},{1,17},{2,18},{3,19},{4,20},{5,21},{6,22},{7,23},{8,24},{9,... | collective-permute-start | bytes 1474568 | tf_op jit(solution)/shard_map/ppermute | solution.py:165
  37.1 8.3 %collective-permute-start.3 = (bf16[4,80,768]{2,1,0:T(8,128)(2,1)S(1)}, bf16[4,80,768]{2,1,0:T(8,128)(2,1)S(1)}, u32[]{:S(2)}, u32[]{:S(2)}) collective-permute-start(bf16[4,80,768]{2,1,0:T(8,128)(2,1)S(1)} %get-tuple-element.556), channel_id=1, source_target_pairs={{0,1},{1,0},{2,3},{3,2},{4,5},{5,4},{6,7},{7,6},{8,9},{9,8},{10,11... | collective-permute-start | bytes 1474568 | tf_op jit(solution)/shard_map/ppermute | solution.py:165
  38.3 20.9 %collective-permute-start.5 = (bf16[4,80,768]{2,1,0:T(8,128)(2,1)S(1)}, bf16[4,80,768]{2,1,0:T(8,128)(2,1)S(1)}, u32[]{:S(2)}, u32[]{:S(2)}) collective-permute-start(bf16[4,80,768]{2,1,0:T(8,128)(2,1)S(1)} %get-tuple-element.556), channel_id=1, source_target_pairs={{0,17},{1,16},{2,19},{3,18},{4,21},{5,20},{6,23},{7,22},{8,25},{9,... | collective-permute-start | bytes 1474568 | tf_op jit(solution)/shard_map/ppermute | solution.py:165
  59.5 18.3 %collective-permute-start.6 = (bf16[4,4,80,768]{3,2,1,0:T(8,128)(2,1)S(1)}, bf16[4,4,80,768]{3,2,1,0:T(8,128)(2,1)}, u32[]{:S(2)}, u32[]{:S(2)}) collective-permute-start(bf16[4,4,80,768]{3,2,1,0:T(8,128)(2,1)S(1)} %pad_maximum_fusion.4), channel_id=1, source_target_pairs={{0,8},{8,0},{16,24},{24,16},{1,9},{9,1},{17,25},{25,17},{2,10},{10... | collective-permute-start | bytes 5898248 | tf_op jit(solution)/shard_map/ppermute | solution.py:157
  314.0 330.6 %reduce-scatter.5.cloned.1.call-start = ((), (), s32[]{:S(2)}) async-start(), calls=%async_computation.3 | async-start | bytes 6082560 | tf_op jit(solution)/shard_map/reduce_scatter | solution.py:448
  363.5 207.3 %copy-start.63 = (bf16[3072]{0:T(1024)(128)(2,1)S(1)}, bf16[3072]{0:T(1024)(128)(2,1)}, u32[]{:S(2)}) copy-start(bf16[3072]{0:T(1024)(128)(2,1)} %get-tuple-element.583) | copy-start | bytes 18436
  363.5 207.3 %copy-start.75 = (bf16[768]{0:T(1024)(128)(2,1)S(1)}, bf16[768]{0:T(1024)(128)(2,1)}, u32[]{:S(2)}) copy-start(bf16[768]{0:T(1024)(128)(2,1)} %get-tuple-element.443) | copy-start | bytes 4612
  363.6 207.3 %copy-start.58 = (bf16[768]{0:T(1024)(128)(2,1)S(1)}, bf16[768]{0:T(1024)(128)(2,1)}, u32[]{:S(2)}) copy-start(bf16[768]{0:T(1024)(128)(2,1)} %get-tuple-element.502) | copy-start | bytes 4612
  363.6 207.4 %copy-start.74 = (bf16[768]{0:T(1024)(128)(2,1)S(1)}, bf16[768]{0:T(1024)(128)(2,1)}, u32[]{:S(2)}) copy-start(bf16[768]{0:T(1024)(128)(2,1)} %get-tuple-element.448) | copy-start | bytes 4612
  363.6 207.5 %copy-start.59 = (bf16[768]{0:T(1024)(128)(2,1)S(1)}, bf16[768]{0:T(1024)(128)(2,1)}, u32[]{:S(2)}) copy-start(bf16[768]{0:T(1024)(128)(2,1)} %get-tuple-element.504) | copy-start | bytes 4612
  590.5 4.3 collective-permute-start.7
  600.6 23.5 %collective-permute-start.8 = (bf16[4,80,768]{2,1,0:T(8,128)(2,1)}, bf16[4,80,768]{2,1,0:T(8,128)(2,1)}, u32[]{:S(2)}, u32[]{:S(2)}) collective-permute-start(bf16[4,80,768]{2,1,0:T(8,128)(2,1)} %get-tuple-element.543), channel_id=1, source_target_pairs={{0,1},{1,0},{2,3},{3,2},{4,5},{5,4},{6,7},{7,6},{8,9},{9,8},{10,11... | collective-permute-start | bytes 1474568 | tf_op jit(solution)/shard_map/ppermute | solution.py:165
  600.6 23.5 %collective-permute-start.10 = (bf16[4,80,768]{2,1,0:T(8,128)(2,1)}, bf16[4,80,768]{2,1,0:T(8,128)(2,1)}, u32[]{:S(2)}, u32[]{:S(2)}) collective-permute-start(bf16[4,80,768]{2,1,0:T(8,128)(2,1)} %get-tuple-element.544), channel_id=1, source_target_pairs={{0,17},{1,16},{2,19},{3,18},{4,21},{5,20},{6,23},{7,22},{8,25},{9,... | collective-permute-start | bytes 1474568 | tf_op jit(solution)/shard_map/ppermute | solution.py:165
  602.9 22.1 %collective-permute-start.9 = (bf16[4,80,768]{2,1,0:T(8,128)(2,1)}, bf16[4,80,768]{2,1,0:T(8,128)(2,1)}, u32[]{:S(2)}, u32[]{:S(2)}) collective-permute-start(bf16[4,80,768]{2,1,0:T(8,128)(2,1)} %get-tuple-element.545), channel_id=1, source_target_pairs={{0,16},{1,17},{2,18},{3,19},{4,20},{5,21},{6,22},{7,23},{8,24},{9,... | collective-permute-start | bytes 1474568 | tf_op jit(solution)/shard_map/ppermute | solution.py:165
  626.9 13.8 %collective-permute-start.11 = (bf16[80,768]{1,0:T(8,128)(2,1)S(1)}, bf16[80,768]{1,0:T(8,128)(2,1)S(1)}, u32[]{:S(2)}, u32[]{:S(2)}) collective-permute-start(bf16[80,768]{1,0:T(8,128)(2,1)S(1)} %get-tuple-element.552), channel_id=1, source_target_pairs={{0,2},{1,3},{2,4},{3,5},{4,6},{5,7},{6,0},{7,1},{8,10},{9,11},{10,... | collective-permute-start | bytes 368648 | tf_op jit(solution)/shard_map/ppermute | solution.py:169
  633.0 7.7 %collective-permute-start.13 = (bf16[80,768]{1,0:T(8,128)(2,1)S(1)}, bf16[80,768]{1,0:T(8,128)(2,1)S(1)}, u32[]{:S(2)}, u32[]{:S(2)}) collective-permute-start(bf16[80,768]{1,0:T(8,128)(2,1)S(1)} %get-tuple-element.553), channel_id=1, source_target_pairs={{0,6},{1,7},{2,0},{3,1},{4,2},{5,3},{6,4},{7,5},{8,14},{9,15},{10,... | collective-permute-start | bytes 368648 | tf_op jit(solution)/shard_map/ppermute | solution.py:169
  633.0 11.4 %collective-permute-start.12 = (bf16[80,768]{1,0:T(8,128)(2,1)S(1)}, bf16[80,768]{1,0:T(8,128)(2,1)S(1)}, u32[]{:S(2)}, u32[]{:S(2)}) collective-permute-start(bf16[80,768]{1,0:T(8,128)(2,1)S(1)} %get-tuple-element.554), channel_id=1, source_target_pairs={{0,4},{1,5},{2,6},{3,7},{4,0},{5,1},{6,2},{7,3},{8,12},{9,13},{10,... | collective-permute-start | bytes 368648 | tf_op jit(solution)/shard_map/ppermute | solution.py:169
  645.6 51.3 %collective-permute-start.14 = (bf16[312,768]{1,0:T(8,128)(2,1)S(1)}, bf16[312,768]{1,0:T(8,128)(2,1)S(1)}, u32[]{:S(2)}, u32[]{:S(2)}) collective-permute-start(bf16[312,768]{1,0:T(8,128)(2,1)S(1)} %get-tuple-element.558), channel_id=1, source_target_pairs={{0,16},{8,24},{16,0},{24,8},{1,17},{9,25},{17,1},{25,9},{2,18},{10... | collective-permute-start | bytes 1437704 | tf_op jit(solution)/shard_map/ppermute | solution.py:157
  699.8 13.6 %collective-permute-start.15 = (bf16[2,312,768]{2,1,0:T(8,128)(2,1)}, bf16[2,312,768]{2,1,0:T(8,128)(2,1)}, u32[]{:S(2)}, u32[]{:S(2)}) collective-permute-start(bf16[2,312,768]{2,1,0:T(8,128)(2,1)} %get-tuple-element.547), channel_id=1, source_target_pairs={{0,8},{8,0},{16,24},{24,16},{1,9},{9,1},{17,25},{25,17},{2,10},{10... | collective-permute-start | bytes 2875400 | tf_op jit(solution)/shard_map/ppermute | solution.py:157
  (82 other events, 1718.8 us)
Sparse Core Ops, SparseCore 0:
  11.9 112.7 all-gather.2
  314.1 116.8 reduce-scatter.2
  436.6 111.8 reduce-scatter.4
